TPU v7x, 512 devices: a whole 4x4x16 slice. The times are simulated.
512 devices in a mesh: seq: 64 (over y_lo, z, core), tensor: 8 (over x, y_hi).
Axes of the slice: x: 4, y: 4 (y_hi: 2, y_lo: 2; y = y_hi * 2 + y_lo), z: 16, core: 2. Of those that a mesh axis runs over, the one named last changes fastest.
Arguments:
- trunk: bfloat16 [2, 4096, 1536], P(None, 'seq', 'tensor'), may hold values from -12 to 12
- w_out: bfloat16 [1536, 1536], P('tensor', 'seq'), may hold values from -1 to 1
- gain_coarse: float32 [1536], replicated, may hold values from 0.1 to 1.9
- w_conv1: bfloat16 [5, 1536, 1536], P(None, 'seq', 'tensor'), may hold values from -0.0625 to 0.0625
- w_up: bfloat16 [1536, 2, 768], P('seq', None, 'tensor'), may hold values from -0.15625 to 0.15625
- skip: bfloat16 [2, 8192, 768], P(None, 'seq', 'tensor'), may hold values from -12 to 12
- gain_fine: float32 [768], replicated, may hold values from 0.1 to 1.9
- w_conv2: bfloat16 [5, 768, 768], P(None, 'seq', 'tensor'), may hold values from -0.09375 to 0.09375
- cotangent: bfloat16 [2, 8192, 768], P(None, 'seq', 'tensor'), may hold values from -6 to 6
Outputs:
- decoded: bfloat16 [2, 8192, 768], P(None, 'seq', 'tensor')
- skip_grad: bfloat16 [2, 8192, 768], P(None, 'seq', 'tensor')
- trunk_grad: bfloat16 [2, 4096, 1536], P(None, 'seq', 'tensor')
All inputs are finite; a program needn't handle non-finite values.
Results may differ from a plain program's by a relative error of at most 0.02.
Values may be sent and summed in bfloat16 or wider, within the bound.
No kernel may reach another device: no remote copies, remote signals or barrier semaphores. Data moves between devices by JAX's collectives and lax.ppermute only.
A program may use at most 64 MiB of HBM per device.

v0:
```python
import jax
import jax.numpy as jnp
from jax import lax
from jax.sharding import PartitionSpec as P

C_COARSE = 1536
C_FINE = 768
EPS = 1e-06


def extended(shard, sides, width):
    for axis, dim in sides:
        size, length = (lax.axis_size(axis), shard.shape[dim])
        up = [(i, (i + 1) % size) for i in range(size - 1)]
        down = [(j, i) for i, j in up]
        last = lax.slice_in_dim(shard, length - width, length, axis=dim)
        leading = lax.slice_in_dim(shard, 0, width, axis=dim)
        before = lax.ppermute(last, axis, up)
        after = lax.ppermute(leading, axis, down)
        shard = jnp.concatenate([before, shard, after], axis=dim)
    return shard


def matmul(left, right):
    return lax.dot_general(
        left, right, (((left.ndim - 1,), (0,)), ((), ())), preferred_element_type=jnp.float32
    )


def matmul_back(left, right):
    return lax.dot_general(
        left,
        right,
        (((left.ndim - 1,), (right.ndim - 1,)), ((), ())),
        preferred_element_type=jnp.float32,
    )


def activate(field, gain):
    scaled = field * lax.rsqrt(jnp.mean(field * field, axis=-1, keepdims=True) + EPS)
    return jax.nn.gelu(scaled * gain)


def widen(field):
    return extended(field, (("seq", 1),), 2)


def spread(field):
    return lax.all_gather(field, "tensor", axis=2, tiled=True)


def conv_rows(total, wide, piece):
    length = wide.shape[1] - 4
    for k in range(5):
        total = total + matmul(wide[:, k : k + length], piece[k])
    return total


def conv_back(wide_grad, piece):
    length = wide_grad.shape[1] - 4
    total = jnp.zeros((wide_grad.shape[0], length, piece.shape[1]), jnp.float32)
    for k in range(5):
        total = total + matmul_back(wide_grad[:, 4 - k : 4 - k + length], piece[k])
    return total


def norm_back(partial_grad, field_full, gain, rank, part):
    field = field_full.astype(jnp.float32)
    start = rank * part
    whole = lax.psum(partial_grad.astype(jnp.bfloat16), "tensor").astype(jnp.float32)

    def apply(value):
        return activate(value, gain)

    _, pull = jax.vjp(apply, field)
    return lax.dynamic_slice_in_dim(pull(whole)[0], start, part, 2)


def per_device(trunk, w_out, gain_coarse, w_conv1, w_up, skip, gain_fine, w_conv2, cotangent):
    rank = lax.axis_index("tensor")
    part_coarse = C_COARSE // lax.axis_size("tensor")
    part_fine = C_FINE // lax.axis_size("tensor")
    seqs = trunk.shape[0]
    slab = trunk.shape[1]
    out_w, up_w, conv2_w = (
        lax.all_gather(w_out, "seq", axis=1, tiled=True),
        lax.all_gather(w_up, "seq", axis=0, tiled=True),
        lax.all_gather(w_conv2, "seq", axis=1, tiled=True),
    )
    partial_proj = matmul(trunk, out_w)
    projected = lax.psum_scatter(
        partial_proj.astype(jnp.bfloat16), "tensor", scatter_dimension=2, tiled=True
    )
    projected_full = lax.all_gather(projected, "tensor", axis=2, tiled=True)
    act_coarse = activate(projected_full.astype(jnp.float32), gain_coarse).astype(jnp.bfloat16)
    coarse_wide = widen(act_coarse)
    empty_coarse = jnp.zeros((seqs, slab, part_coarse), jnp.float32)
    mixed_coarse = conv_rows(
        empty_coarse, coarse_wide, lax.all_gather(w_conv1, "seq", axis=1, tiled=True)
    )
    lifted = (projected.astype(jnp.float32) + mixed_coarse).astype(jnp.bfloat16)
    lifted_full = spread(lifted)
    upper = matmul(lifted_full, up_w).reshape(seqs, 2 * slab, part_fine)
    merged = (upper + skip.astype(jnp.float32)).astype(jnp.bfloat16)
    merged_full = spread(merged)
    act_fine = activate(merged_full.astype(jnp.float32), gain_fine).astype(jnp.bfloat16)
    fine_wide = widen(act_fine)
    empty_fine = jnp.zeros((seqs, 2 * slab, part_fine), jnp.float32)
    mixed_fine = conv_rows(empty_fine, fine_wide, conv2_w)
    decoded = (merged.astype(jnp.float32) + mixed_fine).astype(jnp.bfloat16)
    cot_wide = widen(cotangent)
    back_fine = conv_back(cot_wide, conv2_w)
    skip_grad = (
        cotangent.astype(jnp.float32)
        + norm_back(back_fine, merged_full, gain_fine, rank, part_fine)
    ).astype(jnp.bfloat16)
    folded = skip_grad.reshape(seqs, slab, 2 * part_fine)
    up_partial = matmul_back(folded, up_w.reshape(up_w.shape[0], 2 * part_fine))
    lifted_grad = lax.psum_scatter(
        up_partial.astype(jnp.bfloat16), "tensor", scatter_dimension=2, tiled=True
    )
    grad_wide = widen(lifted_grad)
    back_coarse = conv_back(grad_wide, lax.all_gather(w_conv1, "seq", axis=1, tiled=True))
    projected_grad = (
        lifted_grad.astype(jnp.float32)
        + norm_back(back_coarse, projected_full, gain_coarse, rank, part_coarse)
    ).astype(jnp.bfloat16)
    grad_full = spread(projected_grad)
    trunk_grad = matmul_back(grad_full, out_w).astype(jnp.bfloat16)
    return (decoded, skip_grad, trunk_grad)


def solution(mesh):
    in_specs = (
        P(None, "seq", "tensor"),
        P("tensor", "seq"),
        P(),
        P(None, "seq", "tensor"),
        P("seq", None, "tensor"),
        P(None, "seq", "tensor"),
        P(),
        P(None, "seq", "tensor"),
        P(None, "seq", "tensor"),
    )
    out_specs = (P(None, "seq", "tensor"), P(None, "seq", "tensor"), P(None, "seq", "tensor"))
    return jax.shard_map(
        per_device, mesh=mesh, in_specs=in_specs, out_specs=out_specs, check_vma=False
    )
```

profile of v0, /device:TPU:32, one launch (start us, length us, event | category | flops | bytes accessed | tf_op | source)
XLA Modules:
  0.0 605.8 jit_solution(13952073995251404903)
XLA Ops:
  8.1 69.1 %all_gather.25 = bf16[192,1536]{0,1:T(8,128)(2,1)S(1)} all-gather(bf16[192,24]{0,1:T(8,128)(2,1)} %param.10), channel_id=1, replica_groups=mesh['seq'=64,'tensor'=8] {'seq'}, dimensions={1}, use_global_device_ids=true | all-gather | bytes 599040 | tf_op jit(solution)/shard_map/all_gather | solution.py:86
  78.1 1.1 reshape.66
  80.6 5.0 collective-permute-start.4
  85.6 1.9 collective-permute-start.5
  88.9 65.4 %all_gather.31 = bf16[5,768,96]{2,0,1:T(8,128)(2,1)S(1)} all-gather(bf16[5,12,96]{2,0,1:T(8,128)(2,1)S(1)} %copy.52), channel_id=1, replica_groups=mesh['seq'=64,'tensor'=8] {'seq'}, dimensions={1}, use_global_device_ids=true | all-gather | bytes 748800 | tf_op jit(solution)/shard_map/all_gather | solution.py:88
  154.3 1.4 fusion.107
  155.8 0.9 copy.76
  157.0 0.9 copy.75
  158.8 0.9 copy.78
  160.6 62.1 %all_gather.29 = bf16[1536,2,96]{2,0,1:T(8,128)(2,1)S(1)} all-gather(bf16[24,2,96]{2,0,1:T(8,128)(2,1)} %copy.46), channel_id=1, replica_groups=mesh['seq'=64,'tensor'=8] {'seq'}, dimensions={0}, use_global_device_ids=true | all-gather | bytes 599040 | tf_op jit(solution)/shard_map/all_gather | solution.py:87
  223.0 1.4 constant_dynamic-update-slice_fusion
  224.4 1.3 fusion.60
  225.7 1.3 fusion.69
  227.1 1.3 fusion.4
  228.3 1.9 fusion.5
  231.3 37.2 %all_gather.26 = bf16[2,64,1536]{1,0,2:T(2,128)(2,1)S(1)} all-gather(bf16[2,64,192]{1,0,2:T(2,128)(2,1)S(1)} %bitcast.93), channel_id=1, replica_groups=mesh['seq'=64,'tensor'=8] {'tensor'}, dimensions={2}, use_global_device_ids=true | all-gather | bytes 442368 | tf_op jit(solution)/shard_map/all_gather | solution.py:94
  269.9 1.0 convert_element_type.67
  271.4 1.1 multiply_convert_fusion.1
  272.6 1.9 collective-permute-start
  274.5 3.6 collective-permute-start.1
  278.2 1.4 fusion.43
  279.6 1.4 fusion.41
  281.0 1.4 fusion.45
  282.5 1.4 fusion.6
  283.9 1.4 fusion.9
  285.5 35.9 %all_gather.28 = bf16[2,64,1536]{1,0,2:T(2,128)(2,1)S(1)} all-gather(bf16[2,64,192]{1,0,2:T(2,128)(2,1)S(1)} %copy.45), channel_id=1, replica_groups=mesh['seq'=64,'tensor'=8] {'tensor'}, dimensions={2}, use_global_device_ids=true | all-gather | bytes 442368 | tf_op jit(solution)/shard_map/all_gather | solution.py:49
  322.6 34.9 %all_gather.30 = bf16[2,128,768]{1,0,2:T(2,128)(2,1)S(1)} all-gather(bf16[2,128,96]{1,0,2:T(2,128)(2,1)S(1)} %copy.50), channel_id=1, replica_groups=mesh['seq'=64,'tensor'=8] {'tensor'}, dimensions={2}, use_global_device_ids=true | all-gather | bytes 442368 | tf_op jit(solution)/shard_map/all_gather | solution.py:49
  358.8 1.9 multiply_reduce_fusion.1
  361.4 1.0 fusion.75
  363.9 1.1 reshape.68
  365.2 1.9 collective-permute-start.2
  367.4 1.6 copy.62
  368.9 3.6 collective-permute-start.3
  372.6 1.2 fusion.56
  373.8 1.2 fusion.10
  375.0 69.0 %reduce-scatter.9.cloned.1.call-done = bf16[192,128]{1,0:T(8,128)(2,1)} async-done(((bf16[1536,128]{1,0:T(8,128)(2,1)}), bf16[192,128]{1,0:T(8,128)(2,1)}) %reduce-scatter.9.cloned.1.call-update) | async-done | bytes 49168
  445.0 1.9 collective-permute-start.6
  447.0 2.6 collective-permute-start.7
  449.5 1.5 fusion.42
  451.1 1.5 fusion.40
  452.6 1.6 fusion.44
  454.2 1.6 fusion
  455.9 2.3 fusion.2
  459.4 99.1 %all-reduce.5.cloned.1.call-done = bf16[2,64,1536]{2,1,0:T(8,128)(2,1)} async-done(((bf16[2,64,1536]{2,1,0:T(8,128)(2,1)}), bf16[2,64,1536]{2,1,0:T(8,128)(2,1)}) %all-reduce.5.cloned.1.call-update) | async-done | bytes 393232 | tf_op jit(solution)/shard_map/psum | solution.py:70
  558.5 1.8 multiply_reduce_fusion
  560.3 1.1 fusion.77
  561.6 36.0 %all_gather.32 = bf16[2,64,1536]{1,0,2:T(2,128)(2,1)S(1)} all-gather(bf16[2,64,192]{1,0,2:T(2,128)(2,1)S(1)} %copy.60), channel_id=1, replica_groups=mesh['seq'=64,'tensor'=8] {'tensor'}, dimensions={2}, use_global_device_ids=true | all-gather | bytes 442368 | tf_op jit(solution)/shard_map/all_gather | solution.py:49
  597.6 1.1 convolution_convert_fusion.2
  (99 shorter events, 16.5 us)
Async XLA Ops:
  8.0 69.1 %copy-start = (bf16[2,64,192]{2,1,0:T(8,128)(2,1)S(1)}, bf16[2,64,192]{2,1,0:T(8,128)(2,1)}, u32[]{:S(2)}) copy-start(bf16[2,64,192]{2,1,0:T(8,128)(2,1)} %param.9) | copy-start | bytes 147460
  8.0 71.9 %copy-start.1 = (bf16[2,128,96]{1,2,0:T(8,128)(2,1)S(1)}, bf16[2,128,96]{1,2,0:T(8,128)(2,1)}, u32[]{:S(2)}) copy-start(bf16[2,128,96]{1,2,0:T(8,128)(2,1)} %param.17) | copy-start | bytes 147460
  8.0 80.3 %copy-start.15 = (bf16[24,2,96]{2,1,0:T(2,128)(2,1)S(1)}, bf16[24,2,96]{2,1,0:T(2,128)(2,1)}, u32[]{:S(2)}) copy-start(bf16[24,2,96]{2,1,0:T(2,128)(2,1)} %param.13) | copy-start | bytes 27652
  8.0 80.9 %copy-start.12 = (bf16[5,12,96]{2,1,0:T(8,128)(2,1)S(1)}, bf16[5,12,96]{2,1,0:T(8,128)(2,1)}, u32[]{:S(2)}) copy-start(bf16[5,12,96]{2,1,0:T(8,128)(2,1)} %param.16) | copy-start | bytes 34564
  8.0 222.3 %reduce-scatter.7.cloned.1.call-start = ((), (), s32[]{:S(2)}) async-start(), calls=%async_computation.5 | async-start | bytes 442368
  79.3 198.9 %all-gather.2.cloned.1.call-start = ((), (), s32[]{:S(2)}) async-start(), calls=%async_computation.2 | async-start | bytes 3993600 | tf_op jit(solution)/shard_map/all_gather | solution.py:99
  79.8 278.9 %all-reduce.3.cloned.1.call-start = ((), (), s32[]{:S(2)}) async-start(), calls=%async_computation.3 | async-start | bytes 786432 | tf_op jit(solution)/shard_map/psum | solution.py:70
  80.6 142.4 %collective-permute-start.4 = (bf16[2,2,96]{1,2,0:T(8,128)(2,1)}, bf16[2,2,96]{1,2,0:T(8,128)(2,1)}, u32[]{:S(2)}, u32[]{:S(2)}) collective-permute-start(bf16[2,2,96]{1,2,0:T(8,128)(2,1)} %get-tuple-element.28), channel_id=1, source_target_pairs={{8,0},{16,8},{24,16},{32,24},{40,32},{48,40},{56,48},{64,56},{72,6... | collective-permute-start | bytes 2312 | tf_op jit(solution)/shard_map/ppermute | solution.py:19
  85.6 138.8 %collective-permute-start.5 = (bf16[2,2,96]{1,2,0:T(8,128)(2,1)}, bf16[2,2,96]{1,2,0:T(8,128)(2,1)}, u32[]{:S(2)}, u32[]{:S(2)}) collective-permute-start(bf16[2,2,96]{1,2,0:T(8,128)(2,1)} %get-tuple-element.29), channel_id=1, source_target_pairs={{0,8},{8,16},{16,24},{24,32},{32,40},{40,48},{48,56},{56,64},{64,7... | collective-permute-start | bytes 2312 | tf_op jit(solution)/shard_map/ppermute | solution.py:18
  159.7 67.3 %copy-start.4 = (bf16[1,768,96]{1,2,0:T(8,128)(2,1)S(1)}, bf16[1,768,96]{1,2,0:T(8,128)(2,1)}, u32[]{:S(2)}) copy-start(bf16[1,768,96]{1,2,0:T(8,128)(2,1)} %copy.75) | copy-start | bytes 442372
  160.4 68.0 %copy-start.2 = (bf16[1,768,96]{1,2,0:T(8,128)(2,1)S(1)}, bf16[1,768,96]{1,2,0:T(8,128)(2,1)}, u32[]{:S(2)}) copy-start(bf16[1,768,96]{1,2,0:T(8,128)(2,1)} %copy.78) | copy-start | bytes 442372
  230.3 213.7 %reduce-scatter.9.cloned.1.call-start = ((), (), s32[]{:S(2)}) async-start(), calls=%async_computation.6 | async-start | bytes 442368
  269.9 4.6 copy-start.16
  270.9 0.5 copy-start.13
  271.4 12.5 %copy-start.9 = (bf16[2,64,192]{2,1,0:T(8,128)(2,1)S(1)}, bf16[2,64,192]{2,1,0:T(8,128)(2,1)}, u32[]{:S(2)}) copy-start(bf16[2,64,192]{2,1,0:T(8,128)(2,1)} %copy.67) | copy-start | bytes 147460
  272.6 7.0 %collective-permute-start = (bf16[2,2,1536]{2,1,0:T(2,128)(2,1)S(1)}, bf16[2,2,1536]{2,1,0:T(2,128)(2,1)S(1)}, u32[]{:S(2)}, u32[]{:S(2)}) collective-permute-start(bf16[2,2,1536]{2,1,0:T(2,128)(2,1)S(1)} %get-tuple-element.24), channel_id=1, source_target_pairs={{0,8},{8,16},{16,24},{24,32},{32,40},{40,48},{48,56},{56,64},{64,7... | collective-permute-start | bytes 36872 | tf_op jit(solution)/shard_map/ppermute | solution.py:18
  274.5 6.5 %collective-permute-start.1 = (bf16[2,2,1536]{2,1,0:T(2,128)(2,1)S(1)}, bf16[2,2,1536]{2,1,0:T(2,128)(2,1)S(1)}, u32[]{:S(2)}, u32[]{:S(2)}) collective-permute-start(bf16[2,2,1536]{2,1,0:T(2,128)(2,1)S(1)} %get-tuple-element.25), channel_id=1, source_target_pairs={{8,0},{16,8},{24,16},{32,24},{40,32},{48,40},{56,48},{64,56},{72,6... | collective-permute-start | bytes 36872 | tf_op jit(solution)/shard_map/ppermute | solution.py:19
  282.5 39.5 %copy-start.10 = (bf16[2,128,96]{1,2,0:T(8,128)(2,1)S(1)}, bf16[2,128,96]{1,2,0:T(8,128)(2,1)}, u32[]{:S(2)}) copy-start(bf16[2,128,96]{1,2,0:T(8,128)(2,1)} %param.14) | copy-start | bytes 147460
  322.0 0.6 copy-start.7
  358.2 0.6 copy-start.18
  362.5 0.6 copy-start.5
  365.1 193.4 %all-reduce.5.cloned.1.call-start = ((), (), s32[]{:S(2)}) async-start(), calls=%async_computation.4 | async-start | bytes 786432 | tf_op jit(solution)/shard_map/psum | solution.py:70
  365.2 7.4 %collective-permute-start.2 = (bf16[2,2,768]{2,1,0:T(2,128)(2,1)S(1)}, bf16[2,2,768]{2,1,0:T(2,128)(2,1)S(1)}, u32[]{:S(2)}, u32[]{:S(2)}) collective-permute-start(bf16[2,2,768]{2,1,0:T(2,128)(2,1)S(1)} %get-tuple-element.22), channel_id=1, source_target_pairs={{0,8},{8,16},{16,24},{24,32},{32,40},{40,48},{48,56},{56,64},{64,7... | collective-permute-start | bytes 18440 | tf_op jit(solution)/shard_map/ppermute | solution.py:18
  368.9 89.3 %collective-permute-start.3 = (bf16[2,2,768]{2,1,0:T(2,128)(2,1)S(1)}, bf16[2,2,768]{2,1,0:T(2,128)(2,1)S(1)}, u32[]{:S(2)}, u32[]{:S(2)}) collective-permute-start(bf16[2,2,768]{2,1,0:T(2,128)(2,1)S(1)} %get-tuple-element.23), channel_id=1, source_target_pairs={{8,0},{16,8},{24,16},{32,24},{40,32},{48,40},{56,48},{64,56},{72,6... | collective-permute-start | bytes 18440 | tf_op jit(solution)/shard_map/ppermute | solution.py:19
  445.0 6.1 collective-permute-start.6
  447.0 5.7 collective-permute-start.7
  452.6 5.6 copy-start.6
  454.2 4.3 copy-start.3
  454.2 4.3 copy-start.8
  454.2 104.3 %copy-start.11 = (f32[1536]{0:T(1024)S(1)}, f32[1536]{0:T(1024)}, u32[]{:S(2)}) copy-start(f32[1536]{0:T(1024)} %param.11) | copy-start | bytes 18436
  454.2 104.3 %copy-start.14 = (f32[2,64]{1,0:T(2,128)S(1)}, f32[2,64]{1,0:T(2,128)}, u32[]{:S(2)}) copy-start(f32[2,64]{1,0:T(2,128)} %copy-done.13) | copy-start | bytes 1540
  455.8 104.5 %copy-start.17 = (f32[2,64]{1,0:T(2,128)S(1)}, f32[2,64]{1,0:T(2,128)}, u32[]{:S(2)}) copy-start(f32[2,64]{1,0:T(2,128)} %copy-done.16) | copy-start | bytes 1540
Sparse Core Ops, SparseCore 0:
  79.4 80.6 reduce-scatter.6
  230.4 92.9 all-reduce.2
  365.2 78.7 reduce-scatter.8
  458.3 100.1 all-reduce.4
Sparse Core Ops, SparseCore 1:
  81.8 117.8 all-gather.1
where the time goes:
time: 607 us; the launch traced here: 606 us
  blocking collectives  341 us (56%)
  waiting for transfers between devices  169 us (28%)
  matrix products  27.6 us (5%)
  starting transfers between devices  22.8 us (4%)
  local copies, waits for them, and re-layouts  20.7 us (3%)
  between operations  15.9 us (3%)
  other arithmetic  9.67 us (2%)
    all_gather x3, blocking collectives, spread(): return lax.all_gather(field, 'tensor', axis=2, tiled=True)  107 us
    psum x2, waiting for transfers between devices, norm_back(): lax.psum(partial_grad.astype(jnp.bfloat16), 'tensor').astype(jnp.float32)  99.1 us
    unnamed x7, waiting for transfers between devices  69.6 us
    all_gather x1, blocking collectives, per_device(): lax.all_gather(w_out, 'seq', axis=1, tiled=True)  69.1 us
    all_gather x1, blocking collectives, per_device(): lax.all_gather(w_conv2, 'seq', axis=1, tiled=True)  65.4 us
    all_gather x1, blocking collectives, per_device(): lax.all_gather(w_up, 'seq', axis=0, tiled=True)  62.1 us
    all_gather x1, blocking collectives, per_device(): projected_full = lax.all_gather(projected, 'tensor', axis=2, tiled=True)  37.2 us
    dot_general x12, matrix products, matmul_back(): lax.dot_general(left, right, (((left.ndim - 1,), (right.ndim - 1,)), ((),...  15.9 us
  transfers between devices with their start and end apart: 13, of which 2 were waited for; matrix products, arithmetic and copies ran while one was open for 7% of the time, Pallas kernels for 0%

commit v1 on v0

--- a/solution.py
+++ b/solution.py
@@ -46,7 +46,9 @@
 
 
 def spread(field):
-    return lax.all_gather(field, "tensor", axis=2, tiled=True)
+    return jnp.concatenate(
+        lax.all_to_all(jnp.stack([field] * lax.axis_size("tensor")), "tensor", 0, 0), axis=2
+    )
 
 
 def conv_rows(total, wide, piece):

time: 607 us -> 631 us (1.040)
  waiting for transfers between devices: 169 us -> 289 us
  blocking collectives: 341 us -> 232 us
  starting transfers between devices: 22.8 us -> 36.4 us
    all_gather x3 -> x0, blocking collectives: 107 us -> none  [spread(): return lax.all_gather(field, 'tensor', axis=2, tiled=True)]
    psum x2, waiting for transfers between devices: 99.1 us -> 188 us  [norm_back(): lax.psum(partial_grad.astype(jnp.bfloat16), 'tensor').astype(jnp.float32)]
    all_to_all x0 -> x3, waiting for transfers between devices: none -> 21.9 us  [spread(): lax.all_to_all(jnp.stack([field] * lax.axis_size('tensor')), 'tensor', 0, 0)]
    all_to_all x0 -> x3, starting transfers between devices: none -> 13.6 us  [spread(): lax.all_to_all(jnp.stack([field] * lax.axis_size('tensor')), 'tensor', 0, 0)]
    unnamed x7, waiting for transfers between devices: 69.6 us -> 78.4 us
    unnamed x56 -> x60, local copies, waits for them, and re-layouts: 15.2 us -> 11.7 us
  transfers between devices with their start and end apart: 13 -> 16, of which waited for: 2 -> 6; matrix products, arithmetic and copies ran while one was open for 7% -> 7% of each run, Pallas kernels for 0% -> 0%
where the time goes in v1:
time: 631 us; the launch traced here: 630 us
  waiting for transfers between devices  289 us (46%)
  blocking collectives  232 us (37%)
  starting transfers between devices  36.4 us (6%)
  matrix products  27.9 us (4%)
  local copies, waits for them, and re-layouts  22 us (3%)
  between operations  15.9 us (3%)
  other arithmetic  6.83 us (1%)
    psum x2, waiting for transfers between devices, norm_back(): lax.psum(partial_grad.astype(jnp.bfloat16), 'tensor').astype(jnp.float32)  188 us
    unnamed x7, waiting for transfers between devices  78.4 us
    all_gather x1, blocking collectives, per_device(): lax.all_gather(w_out, 'seq', axis=1, tiled=True)  69.1 us
    all_gather x1, blocking collectives, per_device(): lax.all_gather(w_conv2, 'seq', axis=1, tiled=True)  65 us
    all_gather x1, blocking collectives, per_device(): lax.all_gather(w_up, 'seq', axis=0, tiled=True)  62.1 us
    all_gather x1, blocking collectives, per_device(): projected_full = lax.all_gather(projected, 'tensor', axis=2, tiled=True)  35.5 us
    all_to_all x3, waiting for transfers between devices, spread(): lax.all_to_all(jnp.stack([field] * lax.axis_size('tensor')), 'tensor', 0, 0)  21.9 us
    dot_general x12, matrix products, matmul_back(): lax.dot_general(left, right, (((left.ndim - 1,), (right.ndim - 1,)), ((),...  17.2 us
  transfers between devices with their start and end apart: 16, of which 6 were waited for; matrix products, arithmetic and copies ran while one was open for 7% of the time, Pallas kernels for 0%

profile of v1, /device:TPU:32, one launch (start us, length us, event | category | flops | bytes accessed | tf_op | source)
XLA Modules:
  0.0 629.5 jit_solution(4065376275041626075)
XLA Ops:
  8.1 69.1 %all_gather.16 = bf16[192,1536]{0,1:T(8,128)(2,1)S(1)} all-gather(bf16[192,24]{0,1:T(8,128)(2,1)} %param.10), channel_id=1, replica_groups=mesh['seq'=64,'tensor'=8] {'seq'}, dimensions={1}, use_global_device_ids=true | all-gather | bytes 599040 | tf_op jit(solution)/shard_map/all_gather | solution.py:88
  78.1 1.1 reshape.96
  80.6 5.0 collective-permute-start.4
  85.6 1.9 collective-permute-start.5
  88.3 65.0 %all_gather.20 = bf16[5,768,96]{2,0,1:T(8,128)(2,1)S(1)} all-gather(bf16[5,12,96]{2,0,1:T(8,128)(2,1)S(1)} %copy.43), channel_id=1, replica_groups=mesh['seq'=64,'tensor'=8] {'seq'}, dimensions={1}, use_global_device_ids=true | all-gather | bytes 748800 | tf_op jit(solution)/shard_map/all_gather | solution.py:90
  153.3 1.4 fusion.114
  154.8 0.9 copy.68
  156.0 0.9 copy.67
  157.0 1.2 fusion.72
  158.2 62.1 %all_gather.19 = bf16[1536,2,96]{2,0,1:T(8,128)(2,1)S(1)} all-gather(bf16[24,2,96]{2,0,1:T(8,128)(2,1)S(1)} %copy.38), channel_id=1, replica_groups=mesh['seq'=64,'tensor'=8] {'seq'}, dimensions={0}, use_global_device_ids=true | all-gather | bytes 599040 | tf_op jit(solution)/shard_map/all_gather | solution.py:89
  220.3 0.9 copy.71
  222.1 1.1 copy.53
  224.3 35.5 %all_gather.17 = bf16[2,64,1536]{1,0,2:T(2,128)(2,1)S(1)} all-gather(bf16[2,64,192]{1,0,2:T(2,128)(2,1)S(1)} %bitcast.112), channel_id=1, replica_groups=mesh['seq'=64,'tensor'=8] {'tensor'}, dimensions={2}, use_global_device_ids=true | all-gather | bytes 442368 | tf_op jit(solution)/shard_map/all_gather | solution.py:96
  261.0 1.9 collective-permute-start
  262.9 3.6 collective-permute-start.1
  266.6 1.4 fusion.49
  268.0 1.4 fusion.47
  269.5 1.5 fusion.51
  270.9 1.4 fusion.6
  272.4 1.4 fusion.9
  274.6 6.7 %all-to-all-start = ((bf16[8,2,64,192]{3,2,1,0:T(8,128)(2,1)}), bf16[8,2,64,192]{3,2,1,0:T(8,128)(2,1)S(1)}, u32[]{:S(2)}, u32[]{:S(2)}) async-start(bf16[8,2,64,192]{3,2,1,0:T(8,128)(2,1)} %stack.6), calls=%async_computation | async-start | bytes 1048576 | tf_op jit(solution)/shard_map/all_to_all | solution.py:50
  281.7 1.6 fusion.4
  283.3 8.1 %all-to-all-done = bf16[8,2,64,192]{3,2,1,0:T(8,128)(2,1)S(1)} async-done(((bf16[8,2,64,192]{3,2,1,0:T(8,128)(2,1)}), bf16[8,2,64,192]{3,2,1,0:T(8,128)(2,1)S(1)}, u32[]{:S(2)}, u32[]{:S(2)}) %all-to-all-start) | async-done | bytes 393248 | tf_op jit(solution)/shard_map/all_to_all | solution.py:50
  292.2 1.3 copy.37
  293.5 1.2 reshape.87
  294.7 1.3 fusion.42
  297.9 3.5 all-to-all-start.1
  301.4 1.3 fusion.67
  302.7 2.0 fusion.5
  304.8 5.4 all-to-all-done.1
  310.7 88.4 %all-reduce.3.cloned.1.call-done = bf16[2,128,768]{2,1,0:T(8,128)(2,1)} async-done(((bf16[2,128,768]{2,1,0:T(8,128)(2,1)}), bf16[2,128,768]{2,1,0:T(8,128)(2,1)}) %all-reduce.3.cloned.1.call-update) | async-done | bytes 393232 | tf_op jit(solution)/shard_map/psum | solution.py:72
  399.2 2.5 multiply_reduce_fusion.1
  402.1 1.3 convolution_convert_fusion
  404.0 1.1 reshape.98
  406.1 1.9 collective-permute-start.2
  408.0 3.8 collective-permute-start.3
  412.4 77.8 %reduce-scatter.9.cloned.1.call-done = bf16[192,128]{1,0:T(8,128)(2,1)} async-done(((bf16[1536,128]{1,0:T(8,128)(2,1)}), bf16[192,128]{1,0:T(8,128)(2,1)}) %reduce-scatter.9.cloned.1.call-update) | async-done | bytes 49168
  491.2 1.9 collective-permute-start.6
  493.2 2.4 collective-permute-start.7
  495.6 1.5 fusion.48
  497.1 1.5 fusion.46
  498.7 1.6 fusion.50
  500.2 1.6 fusion
  501.8 2.3 fusion.2
  504.8 100.0 %all-reduce.5.cloned.1.call-done = bf16[2,64,1536]{2,1,0:T(8,128)(2,1)} async-done(((bf16[2,64,1536]{2,1,0:T(8,128)(2,1)}), bf16[2,64,1536]{2,1,0:T(8,128)(2,1)}) %all-reduce.5.cloned.1.call-update) | async-done | bytes 393232 | tf_op jit(solution)/shard_map/psum | solution.py:72
  604.8 1.8 multiply_reduce_fusion
  607.7 3.5 all-to-all-start.2
  612.4 8.4 %all-to-all-done.2 = bf16[8,2,64,192]{3,2,1,0:T(8,128)(2,1)S(1)} async-done(((bf16[8,2,64,192]{3,2,1,0:T(8,128)(2,1)}), bf16[8,2,64,192]{3,2,1,0:T(8,128)(2,1)S(1)}, u32[]{:S(2)}, u32[]{:S(2)}) %all-to-all-start.2) | async-done | bytes 393248 | tf_op jit(solution)/shard_map/all_to_all | solution.py:50
  (112 shorter events, 18.8 us)
Async XLA Ops:
  8.0 69.1 %copy-start = (bf16[2,64,192]{2,1,0:T(8,128)(2,1)S(1)}, bf16[2,64,192]{2,1,0:T(8,128)(2,1)}, u32[]{:S(2)}) copy-start(bf16[2,64,192]{2,1,0:T(8,128)(2,1)} %param.9) | copy-start | bytes 147460
  8.0 71.8 %copy-start.1 = (bf16[2,128,96]{1,2,0:T(8,128)(2,1)S(1)}, bf16[2,128,96]{1,2,0:T(8,128)(2,1)}, u32[]{:S(2)}) copy-start(bf16[2,128,96]{1,2,0:T(8,128)(2,1)} %param.17) | copy-start | bytes 147460
  8.0 80.2 %copy-start.18 = (bf16[24,2,96]{2,1,0:T(2,128)(2,1)S(1)}, bf16[24,2,96]{2,1,0:T(2,128)(2,1)}, u32[]{:S(2)}) copy-start(bf16[24,2,96]{2,1,0:T(2,128)(2,1)} %param.13) | copy-start | bytes 27652
  8.0 80.2 %copy-start.16 = (bf16[5,12,96]{2,1,0:T(8,128)(2,1)S(1)}, bf16[5,12,96]{2,1,0:T(8,128)(2,1)}, u32[]{:S(2)}) copy-start(bf16[5,12,96]{2,1,0:T(8,128)(2,1)} %param.16) | copy-start | bytes 34564
  8.0 215.2 %reduce-scatter.7.cloned.1.call-start = ((), (), s32[]{:S(2)}) async-start(), calls=%async_computation.8 | async-start | bytes 442368
  79.3 187.3 %all-gather.2.cloned.1.call-start = ((), (), s32[]{:S(2)}) async-start(), calls=%async_computation.5 | async-start | bytes 3993600 | tf_op jit(solution)/shard_map/all_gather | solution.py:101
  80.6 142.7 %collective-permute-start.4 = (bf16[2,2,96]{1,2,0:T(8,128)(2,1)S(1)}, bf16[2,2,96]{1,2,0:T(8,128)(2,1)S(1)}, u32[]{:S(2)}, u32[]{:S(2)}) collective-permute-start(bf16[2,2,96]{1,2,0:T(8,128)(2,1)S(1)} %get-tuple-element.28), channel_id=1, source_target_pairs={{8,0},{16,8},{24,16},{32,24},{40,32},{48,40},{56,48},{64,56},{72,6... | collective-permute-start | bytes 2312 | tf_op jit(solution)/shard_map/ppermute | solution.py:19
  85.6 215.8 %collective-permute-start.5 = (bf16[2,2,96]{1,2,0:T(8,128)(2,1)}, bf16[2,2,96]{1,2,0:T(8,128)(2,1)}, u32[]{:S(2)}, u32[]{:S(2)}) collective-permute-start(bf16[2,2,96]{1,2,0:T(8,128)(2,1)} %get-tuple-element.29), channel_id=1, source_target_pairs={{0,8},{8,16},{16,24},{24,32},{32,40},{40,48},{48,56},{56,64},{64,7... | collective-permute-start | bytes 2312 | tf_op jit(solution)/shard_map/ppermute | solution.py:18
  156.0 104.5 %copy-start.15 = (f32[1536]{0:T(1024)S(1)}, f32[1536]{0:T(1024)}, u32[]{:S(2)}) copy-start(f32[1536]{0:T(1024)} %param.11) | copy-start | bytes 18436
  223.2 1.0 copy-start.11
  260.6 11.8 %copy-start.19 = (f32[2,64]{1,0:T(2,128)}, f32[2,64]{1,0:T(2,128)S(1)}, u32[]{:S(2)}) copy-start(f32[2,64]{1,0:T(2,128)S(1)} %multiply_reduce_fusion.3) | copy-start | bytes 1540
  261.0 7.0 %collective-permute-start = (bf16[2,2,1536]{2,1,0:T(2,128)(2,1)S(1)}, bf16[2,2,1536]{2,1,0:T(2,128)(2,1)S(1)}, u32[]{:S(2)}, u32[]{:S(2)}) collective-permute-start(bf16[2,2,1536]{2,1,0:T(2,128)(2,1)S(1)} %get-tuple-element.24), channel_id=1, source_target_pairs={{0,8},{8,16},{16,24},{24,32},{32,40},{40,48},{48,56},{56,64},{64,7... | collective-permute-start | bytes 36872 | tf_op jit(solution)/shard_map/ppermute | solution.py:18
  262.9 6.5 %collective-permute-start.1 = (bf16[2,2,1536]{2,1,0:T(2,128)(2,1)S(1)}, bf16[2,2,1536]{2,1,0:T(2,128)(2,1)S(1)}, u32[]{:S(2)}, u32[]{:S(2)}) collective-permute-start(bf16[2,2,1536]{2,1,0:T(2,128)(2,1)S(1)} %get-tuple-element.25), channel_id=1, source_target_pairs={{8,0},{16,8},{24,16},{32,24},{40,32},{48,40},{56,48},{64,56},{72,6... | collective-permute-start | bytes 36872 | tf_op jit(solution)/shard_map/ppermute | solution.py:19
  269.5 11.8 %copy-start.7 = (bf16[1,768,96]{1,2,0:T(8,128)(2,1)S(1)}, bf16[1,768,96]{1,2,0:T(8,128)(2,1)}, u32[]{:S(2)}) copy-start(bf16[1,768,96]{1,2,0:T(8,128)(2,1)} %copy.68) | copy-start | bytes 442372
  269.5 11.8 %copy-start.12 = (bf16[2,130,96]{1,2,0:T(8,128)(2,1)S(1)}, bf16[2,130,96]{1,2,0:T(8,128)(2,1)}, u32[]{:S(2)}) copy-start(bf16[2,130,96]{1,2,0:T(8,128)(2,1)} %copy-done.11) | copy-start | bytes 149764
  274.6 16.8 %all-to-all-start = ((bf16[8,2,64,192]{3,2,1,0:T(8,128)(2,1)}), bf16[8,2,64,192]{3,2,1,0:T(8,128)(2,1)S(1)}, u32[]{:S(2)}, u32[]{:S(2)}) async-start(bf16[8,2,64,192]{3,2,1,0:T(8,128)(2,1)} %stack.6), calls=%async_computation | async-start | bytes 1048576 | tf_op jit(solution)/shard_map/all_to_all | solution.py:50
  291.4 0.8 copy-start.2
  294.7 8.0 %copy-start.3 = (bf16[1,768,96]{1,2,0:T(8,128)(2,1)S(1)}, bf16[1,768,96]{1,2,0:T(8,128)(2,1)}, u32[]{:S(2)}) copy-start(bf16[1,768,96]{1,2,0:T(8,128)(2,1)} %copy.70) | copy-start | bytes 442372
  297.0 7.8 %copy-start.13 = (bf16[2,128,96]{1,2,0:T(8,128)(2,1)}, bf16[2,128,96]{1,2,0:T(8,128)(2,1)S(1)}, u32[]{:S(2)}) copy-start(bf16[2,128,96]{1,2,0:T(8,128)(2,1)S(1)} %add_convert_fusion) | copy-start | bytes 147460
  297.0 102.1 %copy-start.17 = (f32[768]{0:T(1024)S(1)}, f32[768]{0:T(1024)}, u32[]{:S(2)}) copy-start(f32[768]{0:T(1024)} %param.15) | copy-start | bytes 9220
  297.9 12.4 %all-to-all-start.1 = ((bf16[8,2,128,96]{2,3,1,0:T(8,128)(2,1)}), bf16[8,2,128,96]{2,3,1,0:T(8,128)(2,1)S(1)}, u32[]{:S(2)}, u32[]{:S(2)}) async-start(bf16[8,2,128,96]{2,3,1,0:T(8,128)(2,1)} %stack.7), calls=%async_computation.1 | async-start | bytes 786432 | tf_op jit(solution)/shard_map/all_to_all | solution.py:50
  301.3 97.8 %all-reduce.3.cloned.1.call-start = ((), (), s32[]{:S(2)}) async-start(), calls=%async_computation.6 | async-start | bytes 786432 | tf_op jit(solution)/shard_map/psum | solution.py:72
  302.7 99.0 %copy-start.10 = (bf16[2,128,96]{2,1,0:T(8,128)(2,1)S(1)}, bf16[2,128,96]{2,1,0:T(8,128)(2,1)}, u32[]{:S(2)}) copy-start(bf16[2,128,96]{2,1,0:T(8,128)(2,1)} %copy.50) | copy-start | bytes 147460
  304.7 185.5 %reduce-scatter.9.cloned.1.call-start = ((), (), s32[]{:S(2)}) async-start(), calls=%async_computation.9 | async-start | bytes 442368
  402.0 4.1 copy-start.9
  405.1 199.7 %all-reduce.5.cloned.1.call-start = ((), (), s32[]{:S(2)}) async-start(), calls=%async_computation.7 | async-start | bytes 786432 | tf_op jit(solution)/shard_map/psum | solution.py:72
  406.1 98.1 %collective-permute-start.2 = (bf16[2,2,768]{2,1,0:T(2,128)(2,1)S(1)}, bf16[2,2,768]{2,1,0:T(2,128)(2,1)S(1)}, u32[]{:S(2)}, u32[]{:S(2)}) collective-permute-start(bf16[2,2,768]{2,1,0:T(2,128)(2,1)S(1)} %get-tuple-element.22), channel_id=1, source_target_pairs={{0,8},{8,16},{16,24},{24,32},{32,40},{40,48},{48,56},{56,64},{64,7... | collective-permute-start | bytes 18440 | tf_op jit(solution)/shard_map/ppermute | solution.py:18
  408.0 203.2 %collective-permute-start.3 = (bf16[2,2,768]{2,1,0:T(2,128)(2,1)S(1)}, bf16[2,2,768]{2,1,0:T(2,128)(2,1)S(1)}, u32[]{:S(2)}, u32[]{:S(2)}) collective-permute-start(bf16[2,2,768]{2,1,0:T(2,128)(2,1)S(1)} %get-tuple-element.23), channel_id=1, source_target_pairs={{8,0},{16,8},{24,16},{32,24},{40,32},{48,40},{56,48},{64,56},{72,6... | collective-permute-start | bytes 18440 | tf_op jit(solution)/shard_map/ppermute | solution.py:19
  491.2 5.9 collective-permute-start.6
  493.2 5.5 collective-permute-start.7
  498.7 5.6 copy-start.8
  500.2 4.3 copy-start.5
  501.8 104.8 %copy-start.20 = (f32[2,64]{1,0:T(2,128)S(1)}, f32[2,64]{1,0:T(2,128)}, u32[]{:S(2)}) copy-start(f32[2,64]{1,0:T(2,128)} %copy-done.19) | copy-start | bytes 1540
  501.8 109.4 %copy-start.6 = (bf16[1,768,96]{1,2,0:T(8,128)(2,1)S(1)}, bf16[1,768,96]{1,2,0:T(8,128)(2,1)}, u32[]{:S(2)}) copy-start(bf16[1,768,96]{1,2,0:T(8,128)(2,1)} %copy.71) | copy-start | bytes 442372
  504.2 107.3 %copy-start.4 = (bf16[1,768,96]{1,2,0:T(8,128)(2,1)S(1)}, bf16[1,768,96]{1,2,0:T(8,128)(2,1)}, u32[]{:S(2)}) copy-start(bf16[1,768,96]{1,2,0:T(8,128)(2,1)} %copy.70) | copy-start | bytes 442372
  504.2 107.3 %copy-start.14 = (bf16[2,128,96]{1,2,0:T(8,128)(2,1)S(1)}, bf16[2,128,96]{1,2,0:T(8,128)(2,1)}, u32[]{:S(2)}) copy-start(bf16[2,128,96]{1,2,0:T(8,128)(2,1)} %copy-done.13) | copy-start | bytes 147460
  607.7 13.1 %all-to-all-start.2 = ((bf16[8,2,64,192]{3,2,1,0:T(8,128)(2,1)}), bf16[8,2,64,192]{3,2,1,0:T(8,128)(2,1)S(1)}, u32[]{:S(2)}, u32[]{:S(2)}) async-start(bf16[8,2,64,192]{3,2,1,0:T(8,128)(2,1)} %stack.8), calls=%async_computation.2 | async-start | bytes 1048576 | tf_op jit(solution)/shard_map/all_to_all | solution.py:50
Sparse Core Ops, SparseCore 0:
  79.4 80.6 reduce-scatter.6
  305.1 94.0 all-reduce.2
  405.3 84.9 reduce-scatter.8
  504.3 100.4 all-reduce.4
Sparse Core Ops, SparseCore 1:
  81.8 117.9 all-gather.1
